TPU v7x, 32 devices: a whole 2x2x4 slice. The times are simulated.
32 devices in a mesh: leaf: 8 (over z, core), sub: 4 (over y, x).
Axes of the slice: x: 2, y: 2, z: 4, core: 2. Of those that a mesh axis runs over, the one named last changes fastest.
Arguments:
- leaf_maps: float32 [32, 256, 1024], P('leaf', 'sub'), may hold values from -8 to 28, as said below
- order_one: int32 [8, 4], replicated, may hold values from 0 to 3, each once within a row
- order_two: int32 [4, 6], replicated, may hold values from 0 to 5, each once within a row
- top_data: float32 [16, 256, 256], P('leaf', 'sub'), may hold values from -6 to 6
Outputs:
- top_map: float32 [16, 256, 2048], P('leaf', 'sub')
- leaf_data: float32 [32, 256, 256], P('leaf', 'sub')
Inputs may be any that keep to these rules, and one draw needn't show every extreme that they name: Each leaf's block of 1024 rows of leaf_maps, read as a 1024 by 1024 matrix, is symmetric and positive definite.
All inputs are finite; a program needn't handle non-finite values. Where the computation divides by a largest or mean magnitude, that divisor is 1e-20 or more.
Results may differ from a plain program's by a relative error of at most 0.0001.
Values sent between devices are 32-bit elements; how exact they have to be, the bound alone decides.
No kernel may reach another device: no remote copies, remote signals or barrier semaphores. Data moves between devices by JAX's collectives and lax.ppermute only.
A program may use at most 64 MiB of HBM per device.

v0:
```python
import jax
import jax.numpy as jnp
from jax import lax
from jax.sharding import PartitionSpec as P

W = 256
K = 256
NS_STEPS = 4


def swapped(value, axis, apart):
    mask = 2**apart
    pairs = [(source, source ^ mask) for source in range(lax.axis_size(axis))]
    return lax.ppermute(value, axis, pairs)


def exact_dot(left_matrix, right_matrix):
    return jnp.dot(
        left_matrix,
        right_matrix,
        precision=lax.Precision.HIGHEST,
        preferred_element_type=jnp.float32,
    )


def interface_inverse(block_rows):
    slot_count, width_local, block_size = block_rows.shape
    full_block = lax.all_gather(block_rows, "sub", axis=1, tiled=True).reshape(
        block_size, block_size
    )
    row_bound = jnp.max(jnp.sum(jnp.abs(full_block), axis=1))
    iterate = jnp.eye(block_size, dtype=jnp.float32) / row_bound
    for iteration in range(NS_STEPS):
        iterate = 2.0 * iterate - exact_dot(exact_dot(full_block, iterate), iterate)
    return iterate


def shards(leaf_maps, order_one, order_two, top_data):
    width_local = leaf_maps.shape[1]
    group_index = lax.axis_index("leaf")
    member_index = lax.axis_index("sub")
    parity = group_index % 2
    is_first = parity == 0
    own_order = order_one[group_index]
    permuted = jnp.take(leaf_maps, own_order, axis=0)
    permuted = jnp.take(permuted.reshape(4, width_local, 4, W), own_order, axis=2).reshape(
        4, width_local, 4 * W
    )
    near_rows = permuted[:3]
    inner_piece = permuted[3]
    other_piece = swapped(inner_piece, "leaf", 0)
    first_piece = jnp.where(is_first, inner_piece, other_piece)
    second_piece = jnp.where(is_first, other_piece, inner_piece)
    block_one = first_piece[:, 3 * W :] + second_piece[:, 3 * W :]
    inverse_one = interface_inverse(block_one[None])
    coupling_one = near_rows[:, :, 3 * W :].reshape(3 * width_local, W)
    scaled_one = exact_dot(coupling_one, inverse_one)
    pieces = (
        lax.all_gather(first_piece[:, : 3 * W], "sub", axis=0, tiled=True),
        lax.all_gather(second_piece[:, : 3 * W], "sub", axis=0, tiled=True),
    )
    piece_rows = pieces[0].shape[0]
    joined = jnp.concatenate([pieces[0], pieces[1]], axis=1)
    coeff_part = scaled_one
    running_sum = exact_dot(coeff_part, joined)
    own_part = jnp.where(is_first, pieces[0], pieces[1]).reshape(piece_rows, 3, W)
    own_part = lax.dynamic_slice_in_dim(own_part, member_index * width_local, width_local, 2)
    kept_columns = own_part.reshape(piece_rows, 3 * width_local)
    product_one = running_sum
    right_one = kept_columns
    own_outer = near_rows[:, :, : 3 * W].reshape(3 * width_local, 3 * W)
    zero_one = jnp.zeros_like(own_outer)
    diagonal_one = jnp.where(
        is_first,
        jnp.concatenate([own_outer, zero_one], axis=1),
        jnp.concatenate([zero_one, own_outer], axis=1),
    )
    merged_one = (diagonal_one - product_one).reshape(3, width_local, 6 * W)
    node_index = group_index // 2
    node_first = node_index % 2 == 0
    node_order = order_two[node_index]
    node_rows = jnp.take(merged_one.reshape(3, width_local, 6, W), node_order, axis=2).reshape(
        3, width_local, 6 * W
    )
    position_table = jnp.sum(
        jnp.arange(6)[:, None] * (node_order[:, None] == jnp.arange(6)[None, :]).astype(jnp.int32),
        axis=0,
    )
    my_positions = jnp.take(position_table, 3 * parity + jnp.arange(3))
    slot_edges = node_order[4:6]
    slot_held = (slot_edges // 3 == parity).astype(jnp.float32)
    slot_piece = jnp.take(node_rows, slot_edges % 3, axis=0) * slot_held[:, None, None]
    node_piece = slot_piece + swapped(slot_piece, "leaf", 0)
    cousin_piece = swapped(node_piece, "leaf", 1)
    first_node = jnp.where(node_first, node_piece, cousin_piece)
    second_node = jnp.where(node_first, cousin_piece, node_piece)
    block_two = first_node[:, :, 4 * W :] + second_node[:, :, 4 * W :]
    inverse_two = interface_inverse(block_two)
    coupling_two = node_rows[:, :, 4 * W :].reshape(3 * width_local, 2 * W)
    scaled_two = exact_dot(coupling_two, inverse_two).reshape(3 * width_local, 2, W)
    top_first = 2 * (group_index % 4)
    pieces = (
        lax.all_gather(first_node[:, :, : 4 * W], "sub", axis=1, tiled=True),
        lax.all_gather(second_node[:, :, : 4 * W], "sub", axis=1, tiled=True),
    )
    piece_rows = pieces[0].shape[1]
    joined = jnp.concatenate([pieces[0], pieces[1]], axis=2)
    coeff_part = scaled_two.reshape(3 * width_local, 2 * piece_rows)
    running_sum = exact_dot(coeff_part, joined.reshape(2 * piece_rows, 8 * W))
    own_part = lax.dynamic_slice_in_dim(joined.reshape(2, piece_rows, 8, W), top_first, 2, 2)
    own_part = lax.dynamic_slice_in_dim(own_part, member_index * width_local, width_local, 3)
    kept_columns = own_part
    node_outer = node_rows[:, :, : 4 * W].reshape(3 * width_local, 4 * W)
    zero_two = jnp.zeros_like(node_outer)
    diagonal_two = jnp.where(
        node_first,
        jnp.concatenate([node_outer, zero_two], axis=1),
        jnp.concatenate([zero_two, node_outer], axis=1),
    )
    top_rows = (diagonal_two - running_sum).reshape(3, width_local, 8 * W)
    node_offset = 4 * (node_index % 2)
    buffer = jnp.zeros((8, width_local, 8 * W), jnp.float32)
    for row_slot in range(3):
        target = node_offset + my_positions[row_slot]
        marker = ((jnp.arange(8) == target) & (my_positions[row_slot] < 4)).astype(jnp.float32)
        buffer = buffer + marker[:, None, None] * top_rows[row_slot][None]
    upper_half = node_index % 2
    outgoing = lax.dynamic_slice_in_dim(buffer, 4 * (1 - upper_half), 4, 0)
    retained = lax.dynamic_slice_in_dim(buffer, 4 * upper_half, 4, 0)
    retained = retained + swapped(outgoing, "leaf", 1)
    outgoing_near = lax.dynamic_slice_in_dim(retained, 2 * (1 - parity), 2, 0)
    own_part = lax.dynamic_slice_in_dim(retained, 2 * parity, 2, 0)
    top_map = own_part + swapped(outgoing_near, "leaf", 0)
    partial_two = exact_dot(
        kept_columns.reshape(2 * W, 2 * width_local), top_data.reshape(2 * width_local, K)
    )
    partial_two = lax.psum(partial_two, "sub")
    spread = lax.dynamic_update_slice_in_dim(
        jnp.zeros((8, width_local, K), jnp.float32), top_data, top_first, 0
    )
    for bit_index in range(2):
        other_sum, other_spread = swapped((partial_two, spread), "leaf", bit_index)
        partial_two = partial_two + other_sum
        spread = spread + other_spread
    inner_two = -exact_dot(inverse_two, partial_two)
    inner_local = lax.dynamic_slice_in_dim(
        inner_two.reshape(2, W, K), member_index * width_local, width_local, 1
    )
    candidates = jnp.concatenate(
        [lax.dynamic_slice_in_dim(spread, node_offset, 4, 0), inner_local], axis=0
    )
    node_data = jnp.take(candidates, my_positions, axis=0)
    partial_one = exact_dot(right_one, node_data.reshape(3 * width_local, K))
    partial_one = lax.psum(partial_one, "sub")
    partial_one = partial_one + swapped(partial_one, "leaf", 0)
    inner_one = -exact_dot(inverse_one, partial_one)
    inner_slice = lax.dynamic_slice_in_dim(inner_one, member_index * width_local, width_local, 0)
    permuted_data = jnp.concatenate([node_data, inner_slice[None]], axis=0)
    restore = (own_order[:, None] == jnp.arange(4)[None, :]).astype(jnp.float32)
    leaf_data = jnp.zeros((4, width_local, K), jnp.float32)
    for position in range(4):
        leaf_data = leaf_data + restore[position][:, None, None] * permuted_data[position][None]
    return (top_map, leaf_data)


def solution(mesh):
    in_specs = (P("leaf", "sub", None), P(), P(), P("leaf", "sub", None))
    out_specs = (P("leaf", "sub", None), P("leaf", "sub", None))
    return jax.shard_map(shards, mesh=mesh, in_specs=in_specs, out_specs=out_specs, check_vma=False)
```

profile of v0, /device:TPU:0, one launch (start us, length us, event | category | flops | bytes accessed | tf_op | source)
XLA Modules:
  0.0 383.9 jit_solution(1197257132475756715)
XLA Ops:
  13.0 10.0 %all-gather = f32[256,256]{1,0:T(8,128)S(1)} all-gather(f32[64,256]{1,0:T(8,128)S(1)} %slice_add_fusion.1), channel_id=2, replica_groups=mesh['leaf'=8,'sub'=4] {'sub'}, dimensions={0}, use_global_device_ids=true | all-gather | bytes 327680 | tf_op jit(solution)/shard_map/all_gather | solution.py:28
  27.6 12.5 %all_gather.20 = f32[256,768]{1,0:T(8,128)S(1)} all-gather(f32[64,768]{1,0:T(8,128)S(1)} %slice.143), channel_id=1, replica_groups=mesh['leaf'=8,'sub'=4] {'sub'}, dimensions={0}, use_global_device_ids=true | all-gather | bytes 983040 | tf_op jit(solution)/shard_map/all_gather | solution.py:60
  40.0 10.2 %all_gather.19 = f32[256,768]{1,0:T(8,128)S(1)} all-gather(f32[64,768]{1,0:T(8,128)S(1)} %slice.142), channel_id=1, replica_groups=mesh['leaf'=8,'sub'=4] {'sub'}, dimensions={0}, use_global_device_ids=true | all-gather | bytes 983040 | tf_op jit(solution)/shard_map/all_gather | solution.py:59
  53.3 2.8 copy.20
  56.1 1.9 gather_fusion.3
  59.1 2.3 collective-permute-done.1
  62.4 1.6 collective-permute-start.2
  64.0 18.3 %collective-permute-done.2 = f32[2,64,1536]{2,1,0:T(8,128)} collective-permute-done((f32[2,64,1536]{2,1,0:T(8,128)}, f32[2,64,1536]{2,1,0:T(8,128)}, u32[]{:S(2)}, u32[]{:S(2)}) %collective-permute-start.2) | collective-permute-done | bytes 786464 | tf_op jit(solution)/shard_map/ppermute | solution.py:14
  85.5 1.9 slice.148
  95.5 16.9 %all-gather.5.cloned.1.call-done = f32[2,256,512]{2,1,0:T(8,128)} async-done(((f32[2,64,512]{2,1,0:T(8,128)}), f32[2,256,512]{2,1,0:T(8,128)}) %all-gather.5.cloned.1.call-update) | async-done | bytes 1048592 | tf_op jit(solution)/shard_map/all_gather | solution.py:28
  115.1 3.1 fusion.2
  118.2 1.8 fusion.7
  120.0 1.8 fusion.45
  121.8 1.8 convolution_subtract_fusion.4
  123.7 1.8 fusion.46
  125.6 1.8 convolution_subtract_fusion.3
  127.4 2.1 fusion.47
  129.5 1.9 convolution_subtract_fusion.2
  132.3 17.2 %all-gather.7.cloned.1.call-done = f32[2,256,1024]{2,1,0:T(8,128)} async-done(((f32[2,64,1024]{2,1,0:T(8,128)}), f32[2,256,1024]{2,1,0:T(8,128)}) %all-gather.7.cloned.1.call-update) | async-done | bytes 2097168 | tf_op jit(solution)/shard_map/all_gather | solution.py:103
  149.5 3.2 constant_dynamic-update-slice_fusion.1
  152.7 34.4 %all-gather.9.cloned.1.call-done = f32[2,256,1024]{2,1,0:T(8,128)} async-done(((f32[2,64,1024]{2,1,0:T(8,128)}), f32[2,256,1024]{2,1,0:T(8,128)}) %all-gather.9.cloned.1.call-update) | async-done | bytes 2097168 | tf_op jit(solution)/shard_map/all_gather | solution.py:104
  187.1 3.2 constant_dynamic-update-slice_fusion
  190.3 7.3 %copy.24 = f32[2,256,2048]{1,0,2:T(2,128)} copy(f32[2,256,2048]{2,1,0:T(8,128)} %constant_dynamic-update-slice_fusion) | data formatting | bytes 8388608 | tf_op jit(solution)/shard_map/reshape | solution.py:110
  200.2 4.7 %convolution_subtract_fusion.1 = f32[192,2048]{1,0:T(8,128)S(1)} fusion(f32[192,512]{1,0:T(8,128)S(1)} %fusion.48, f32[512,2048]{1,0:T(8,128)} %bitcast.129, f32[192,1024]{1,0:T(8,128)S(1)} %bitcast.131, pred[]{:T(512)S(6)} %eq.94), kind=kOutput, calls=%fused_computation.8 | convolution fusion | flops 2416705536 | bytes 6946817 | tf_op jit(solution)/shard_map/dot_general | solution.py:18
  205.8 39.8 %all-reduce.7.cloned.1.call-done = f32[512,256]{1,0:T(8,128)} async-done(((f32[512,256]{1,0:T(8,128)}), f32[512,256]{1,0:T(8,128)}) %all-reduce.7.cloned.1.call-update) | async-done | bytes 524304 | tf_op jit(solution)/shard_map/psum | solution.py:137
  245.6 1.8 multiply_add_fusion
  258.4 51.7 %collective-permute-done.6 = f32[8,64,256]{2,1,0:T(8,128)} collective-permute-done((f32[8,64,256]{2,1,0:T(8,128)}, f32[8,64,256]{2,1,0:T(8,128)}, u32[]{:S(2)}, u32[]{:S(2)}) %collective-permute-start.6) | collective-permute-done | bytes 524320 | tf_op jit(solution)/shard_map/ppermute | solution.py:14
  311.1 9.7 %collective-permute-done.8 = f32[512,256]{1,0:T(8,128)} collective-permute-done((f32[512,256]{1,0:T(8,128)}, f32[512,256]{1,0:T(8,128)}, u32[]{:S(2)}, u32[]{:S(2)}) %collective-permute-start.8) | collective-permute-done | bytes 524320 | tf_op jit(solution)/shard_map/ppermute | solution.py:14
  320.9 2.2 convolution_negate_fusion
  325.3 43.1 %all-reduce.9.cloned.1.call-done = f32[256,256]{1,0:T(8,128)} async-done(((f32[256,256]{1,0:T(8,128)}), f32[256,256]{1,0:T(8,128)}) %all-reduce.9.cloned.1.call-update) | async-done | bytes 262160 | tf_op jit(solution)/shard_map/psum | solution.py:154
  368.4 2.5 dynamic-slice_add_fusion
  375.1 2.3 dynamic-slice_add_fusion.1
  (135 shorter events, 46.4 us)
Async XLA Ops:
  7.2 1.2 copy-start
  7.2 105.2 %all-gather.5.cloned.1.call-start = ((), (), s32[]{:S(2)}) async-start(), calls=%async_computation | async-start | bytes 1310720 | tf_op jit(solution)/shard_map/all_gather | solution.py:28
  10.3 2.6 collective-permute-start
  26.8 23.8 %copy-start.8 = (f32[3,64,768]{2,1,0:T(8,128)S(1)}, f32[3,64,768]{2,1,0:T(8,128)}, u32[]{:S(2)}) copy-start(f32[3,64,768]{2,1,0:T(8,128)} %slice.137) | copy-start | bytes 1769476
  50.2 1.6 copy-start.5
  58.3 37.3 %copy-start.4 = (f32[3,64,1536]{2,1,0:T(8,128)}, f32[3,64,1536]{2,1,0:T(8,128)S(1)}, u32[]{:S(2)}) copy-start(f32[3,64,1536]{2,1,0:T(8,128)S(1)} %broadcast_select_fusion) | copy-start | bytes 3538948
  59.0 2.4 collective-permute-start.1
  62.4 19.9 %collective-permute-start.2 = (f32[2,64,1536]{2,1,0:T(8,128)}, f32[2,64,1536]{2,1,0:T(8,128)}, u32[]{:S(2)}, u32[]{:S(2)}) collective-permute-start(f32[2,64,1536]{2,1,0:T(8,128)} %fusion.90), channel_id=1, source_target_pairs={{0,8},{4,12},{8,0},{12,4},{16,24},{20,28},{24,16},{28,20},{1,9},{5... | collective-permute-start | bytes 2359304 | tf_op jit(solution)/shard_map/ppermute | solution.py:14
  83.8 0.9 copy-start.7
  83.8 4.5 %copy-start.9 = (f32[2,64,256]{2,1,0:T(8,128)S(1)}, f32[2,64,256]{2,1,0:T(8,128)}, u32[]{:S(2)}) copy-start(f32[2,64,256]{2,1,0:T(8,128)} %param.7) | copy-start | bytes 393220
  85.5 64.0 %all-gather.7.cloned.1.call-start = ((), (), s32[]{:S(2)}) async-start(), calls=%async_computation.1 | async-start | bytes 2621440 | tf_op jit(solution)/shard_map/all_gather | solution.py:103
  87.5 99.7 %all-gather.9.cloned.1.call-start = ((), (), s32[]{:S(2)}) async-start(), calls=%async_computation.2 | async-start | bytes 2621440 | tf_op jit(solution)/shard_map/all_gather | solution.py:104
  89.0 162.5 %collective-permute-start.5 = (f32[8,64,256]{2,1,0:T(8,128)}, f32[8,64,256]{2,1,0:T(8,128)}, u32[]{:S(2)}, u32[]{:S(2)}) collective-permute-start(f32[8,64,256]{2,1,0:T(8,128)} %constant_dynamic-update-slice_fusion.2), channel_id=1, source_target_pairs={{0,4},{4,0},{8,12},{12,8},{16,20},{20,16},{24,28},{28,24},{1,5},{5... | collective-permute-start | bytes 1572872 | tf_op jit(solution)/shard_map/ppermute | solution.py:14
  95.3 150.4 %all-reduce.7.cloned.1.call-start = ((), (), s32[]{:S(2)}) async-start(), calls=%async_computation.3 | async-start | bytes 1048576 | tf_op jit(solution)/shard_map/psum | solution.py:137
  115.1 4.9 %copy-start.2 = (f32[2,256,512]{2,1,0:T(8,128)S(1)}, f32[2,256,512]{2,1,0:T(8,128)}, u32[]{:S(2)}) copy-start(f32[2,256,512]{2,1,0:T(8,128)} %all-gather.5.cloned.1.call-done) | copy-start | bytes 3145732
  129.5 1.9 slice-start
  197.6 2.6 slice-start.1
  200.1 168.3 %all-reduce.9.cloned.1.call-start = ((), (), s32[]{:S(2)}) async-start(), calls=%async_computation.4 | async-start | bytes 524288 | tf_op jit(solution)/shard_map/psum | solution.py:154
  245.6 8.0 %collective-permute-start.7 = (f32[512,256]{1,0:T(8,128)}, f32[512,256]{1,0:T(8,128)S(1)}, u32[]{:S(2)}, u32[]{:S(2)}) collective-permute-start(f32[512,256]{1,0:T(8,128)} %all-reduce.7.cloned.1.call-done), channel_id=1, source_target_pairs={{0,4},{4,0},{8,12},{12,8},{16,20},{20,16},{24,28},{28,24},{1,5},{5... | collective-permute-start | bytes 1572872 | tf_op jit(solution)/shard_map/ppermute | solution.py:14
  247.4 2.6 copy-start.3
  247.5 6.2 %copy-start.10 = (f32[512,256]{1,0:T(8,128)S(1)}, f32[512,256]{1,0:T(8,128)}, u32[]{:S(2)}) copy-start(f32[512,256]{1,0:T(8,128)} %all-reduce.7.cloned.1.call-done) | copy-start | bytes 1572868
  247.5 8.5 %copy-start.6 = (f32[256,768]{1,0:T(8,128)S(1)}, f32[256,768]{1,0:T(8,128)}, u32[]{:S(2)}) copy-start(f32[256,768]{1,0:T(8,128)} %copy-done.5) | copy-start | bytes 2359300
  250.0 118.4 %collective-permute-start.3 = (f32[4,64,2048]{2,1,0:T(8,128)}, f32[4,64,2048]{2,1,0:T(8,128)}, u32[]{:S(2)}, u32[]{:S(2)}) collective-permute-start(f32[4,64,2048]{2,1,0:T(8,128)} %constant_dynamic-slice_fusion.3), channel_id=1, source_target_pairs={{0,8},{4,12},{8,0},{12,4},{16,24},{20,28},{24,16},{28,20},{1,9},{5... | collective-permute-start | bytes 6291464 | tf_op jit(solution)/shard_map/ppermute | solution.py:14
  253.1 57.0 %collective-permute-start.6 = (f32[8,64,256]{2,1,0:T(8,128)}, f32[8,64,256]{2,1,0:T(8,128)}, u32[]{:S(2)}, u32[]{:S(2)}) collective-permute-start(f32[8,64,256]{2,1,0:T(8,128)} %add_dynamic-update-slice_fusion), channel_id=1, source_target_pairs={{0,8},{4,12},{8,0},{12,4},{16,24},{20,28},{24,16},{28,20},{1,9},{5... | collective-permute-start | bytes 1572872 | tf_op jit(solution)/shard_map/ppermute | solution.py:14
  254.5 66.3 %collective-permute-start.8 = (f32[512,256]{1,0:T(8,128)}, f32[512,256]{1,0:T(8,128)}, u32[]{:S(2)}, u32[]{:S(2)}) collective-permute-start(f32[512,256]{1,0:T(8,128)} %add.281), channel_id=1, source_target_pairs={{0,8},{4,12},{8,0},{12,4},{16,24},{20,28},{24,16},{28,20},{1,9},{5... | collective-permute-start | bytes 1572872 | tf_op jit(solution)/shard_map/ppermute | solution.py:14
  368.4 4.1 %collective-permute-start.9 = (f32[256,256]{1,0:T(8,128)}, f32[256,256]{1,0:T(8,128)}, u32[]{:S(2)}, u32[]{:S(2)}) collective-permute-start(f32[256,256]{1,0:T(8,128)} %all-reduce.9.cloned.1.call-done), channel_id=1, source_target_pairs={{0,4},{4,0},{8,12},{12,8},{16,20},{20,16},{24,28},{28,24},{1,5},{5... | collective-permute-start | bytes 786440 | tf_op jit(solution)/shard_map/ppermute | solution.py:14
  371.9 3.1 collective-permute-start.4
  372.5 4.9 %copy-start.1 = (f32[4,64,1024]{2,1,0:T(8,128)S(1)}, f32[4,64,1024]{2,1,0:T(8,128)}, u32[]{:S(2)}) copy-start(f32[4,64,1024]{2,1,0:T(8,128)} %param.4) | copy-start | bytes 3145732
Sparse Core Ops, SparseCore 0:
  85.6 26.7 all-gather.4
  114.3 35.1 all-gather.6
  151.9 35.1 all-gather.8
  200.2 45.3 all-reduce.6
  325.3 43.0 all-reduce.8
where the time goes:
time: 385 us; the launch traced here: 384 us
  waiting for transfers between devices  234 us (61%)
  local copies, waits for them, and re-layouts  38.4 us (10%)
  matrix products  32.8 us (9%)
  blocking collectives  32.7 us (8%)
  other arithmetic  19.8 us (5%)
  between operations  19.8 us (5%)
  starting transfers between devices  6.62 us (2%)
    ppermute x10, waiting for transfers between devices, swapped(): return lax.ppermute(value, axis, pairs)  82.2 us
    psum x1, waiting for transfers between devices, shards(): partial_one = lax.psum(partial_one, 'sub')  43.1 us
    psum x1, waiting for transfers between devices, shards(): partial_two = lax.psum(partial_two, 'sub')  39.8 us
    all_gather x1, waiting for transfers between devices, shards(): lax.all_gather(second_node[:, :, :4 * W], 'sub', axis=1, tiled=True)  34.4 us
    dot_general x24, matrix products, exact_dot(): jnp.dot(left_matrix, right_matrix, precision=lax.Precision.HIGHEST, prefe...  32.8 us
    all_gather x1, waiting for transfers between devices, shards(): lax.all_gather(first_node[:, :, :4 * W], 'sub', axis=1, tiled=True)  17.2 us
    all_gather x1, waiting for transfers between devices, interface_inverse(): lax.all_gather(block_rows, 'sub', axis=1, tiled=True)  16.9 us
    all_gather x1, blocking collectives, shards(): lax.all_gather(second_piece[:, :3 * W], 'sub', axis=0, tiled=True)  12.5 us
  transfers between devices with their start and end apart: 15, of which 10 were waited for; matrix products, arithmetic and copies ran while one was open for 18% of the time, Pallas kernels for 0%

commit v1 on v0

--- a/solution.py
+++ b/solution.py
@@ -6,6 +6,27 @@
 W = 256
 K = 256
 NS_STEPS = 4
+
+
+def gather_around(shard, axis, dim):
+    count, index, rows = (lax.axis_size(axis), lax.axis_index(axis), shard.shape[dim])
+    ahead = [(i, (i + 1) % count) for i in range(count)]
+    behind = [(i, (i - 1) % count) for i in range(count)]
+    out = jnp.zeros((*shard.shape[:dim], count * rows, *shard.shape[dim + 1 :]), shard.dtype)
+    out = lax.dynamic_update_slice_in_dim(out, shard, index * rows, axis=dim)
+    from_left = from_right = shard
+    halfway = count // 2
+    for step in range(1, halfway + 1):
+        from_left = lax.ppermute(from_left, axis, ahead)
+        out = lax.dynamic_update_slice_in_dim(
+            out, from_left, (index - step) % count * rows, axis=dim
+        )
+        if step < count - halfway:
+            from_right = lax.ppermute(from_right, axis, behind)
+            out = lax.dynamic_update_slice_in_dim(
+                out, from_right, (index + step) % count * rows, axis=dim
+            )
+    return out
 
 
 def swapped(value, axis, apart):
@@ -25,9 +46,7 @@
 
 def interface_inverse(block_rows):
     slot_count, width_local, block_size = block_rows.shape
-    full_block = lax.all_gather(block_rows, "sub", axis=1, tiled=True).reshape(
-        block_size, block_size
-    )
+    full_block = gather_around(block_rows, "sub", 1).reshape(block_size, block_size)
     row_bound = jnp.max(jnp.sum(jnp.abs(full_block), axis=1))
     iterate = jnp.eye(block_size, dtype=jnp.float32) / row_bound
     for iteration in range(NS_STEPS):

time: 385 us -> 364 us (0.945)
  waiting for transfers between devices: 234 us -> 211 us
  starting transfers between devices: 6.62 us -> 15.7 us
  blocking collectives: 32.7 us -> 23.9 us
    ppermute x0 -> x6, waiting for transfers between devices: none -> 18.2 us  [the longest x4 13.6 us: gather_around(): from_left = lax.ppermute(from_left, axis, ahead)]
    all_gather x1, waiting for transfers between devices: 17.2 us -> 0.02 us  [shards(): lax.all_gather(first_node[:, :, :4 * W], 'sub', axis=1, tiled=True)]
    all_gather x1 -> x0, waiting for transfers between devices: 16.9 us -> none  [interface_inverse(): lax.all_gather(block_rows, 'sub', axis=1, tiled=True)]
    all_gather x1 -> x0, blocking collectives: 10 us -> none  [interface_inverse(): lax.all_gather(block_rows, 'sub', axis=1, tiled=True)]
    ppermute x0 -> x6, starting transfers between devices: none -> 9.11 us  [the longest x2 5.72 us: gather_around(): from_right = lax.ppermute(from_right, axis, behind)]
    all_gather x1, waiting for transfers between devices: 34.4 us -> 27.6 us  [shards(): lax.all_gather(second_node[:, :, :4 * W], 'sub', axis=1, tiled=True)]
  transfers between devices with their start and end apart: 15 -> 20, of which waited for: 10 -> 12; matrix products, arithmetic and copies ran while one was open for 18% -> 19% of each run, Pallas kernels for 0% -> 0%
where the time goes in v1:
time: 364 us; the launch traced here: 363 us
  waiting for transfers between devices  211 us (58%)
  local copies, waits for them, and re-layouts  40.9 us (11%)
  matrix products  31.5 us (9%)
  blocking collectives  23.9 us (7%)
  other arithmetic  20.5 us (6%)
  between operations  19.5 us (5%)
  starting transfers between devices  15.7 us (4%)
    ppermute x10, waiting for transfers between devices, swapped(): return lax.ppermute(value, axis, pairs)  82.2 us
    psum x1, waiting for transfers between devices, shards(): partial_one = lax.psum(partial_one, 'sub')  43.1 us
    psum x1, waiting for transfers between devices, shards(): partial_two = lax.psum(partial_two, 'sub')  39.9 us
    dot_general x24, matrix products, exact_dot(): jnp.dot(left_matrix, right_matrix, precision=lax.Precision.HIGHEST, prefe...  31.5 us
    all_gather x1, waiting for transfers between devices, shards(): lax.all_gather(second_node[:, :, :4 * W], 'sub', axis=1, tiled=True)  27.6 us
    ppermute x4, waiting for transfers between devices, gather_around(): from_left = lax.ppermute(from_left, axis, ahead)  13.6 us
    all_gather x1, blocking collectives, shards(): lax.all_gather(second_piece[:, :3 * W], 'sub', axis=0, tiled=True)  12.2 us
    all_gather x1, blocking collectives, shards(): lax.all_gather(first_piece[:, :3 * W], 'sub', axis=0, tiled=True)  11.7 us
  transfers between devices with their start and end apart: 20, of which 12 were waited for; matrix products, arithmetic and copies ran while one was open for 19% of the time, Pallas kernels for 0%

profile of v1, /device:TPU:0, one launch (start us, length us, event | category | flops | bytes accessed | tf_op | source)
XLA Modules:
  0.0 363.1 jit_solution(9465776020700835497)
XLA Ops:
  13.1 3.5 collective-permute-start.2
  16.7 12.2 %all_gather.13 = f32[256,768]{1,0:T(8,128)S(1)} all-gather(f32[64,768]{1,0:T(8,128)S(1)} %slice.143), channel_id=1, replica_groups=mesh['leaf'=8,'sub'=4] {'sub'}, dimensions={0}, use_global_device_ids=true | all-gather | bytes 983040 | tf_op jit(solution)/shard_map/all_gather | solution.py:79
  28.9 11.7 %all_gather.12 = f32[256,768]{1,0:T(8,128)S(1)} all-gather(f32[64,768]{1,0:T(8,128)S(1)} %slice.142), channel_id=1, replica_groups=mesh['leaf'=8,'sub'=4] {'sub'}, dimensions={0}, use_global_device_ids=true | all-gather | bytes 983040 | tf_op jit(solution)/shard_map/all_gather | solution.py:78
  42.3 3.4 collective-permute-done.3
  53.4 2.8 copy.22
  56.2 1.9 gather_fusion.3
  59.2 2.3 collective-permute-done.4
  64.1 18.3 %collective-permute-done.5 = f32[2,64,1536]{2,1,0:T(8,128)} collective-permute-done((f32[2,64,1536]{2,1,0:T(8,128)}, f32[2,64,1536]{2,1,0:T(8,128)}, u32[]{:S(2)}, u32[]{:S(2)}) %collective-permute-start.5) | collective-permute-done | bytes 786464 | tf_op jit(solution)/shard_map/ppermute | solution.py:35
  82.4 2.4 broadcast_select_fusion.3
  93.9 2.2 collective-permute-start.7
  97.2 5.8 %collective-permute-done.6 = f32[2,64,512]{2,1,0:T(8,128)} collective-permute-done((f32[2,64,512]{2,1,0:T(8,128)}, f32[2,64,512]{2,1,0:T(8,128)}, u32[]{:S(2)}, u32[]{:S(2)}) %collective-permute-start.6) | collective-permute-done | bytes 262176 | tf_op jit(solution)/shard_map/ppermute | solution.py:20
  107.1 4.6 %collective-permute-done.7 = f32[2,64,512]{2,1,0:T(8,128)} collective-permute-done((f32[2,64,512]{2,1,0:T(8,128)}, f32[2,64,512]{2,1,0:T(8,128)}, u32[]{:S(2)}, u32[]{:S(2)}) %collective-permute-start.7) | collective-permute-done | bytes 262176 | tf_op jit(solution)/shard_map/ppermute | solution.py:25
  112.7 4.3 %collective-permute-done.8 = f32[2,64,512]{2,1,0:T(8,128)} collective-permute-done((f32[2,64,512]{2,1,0:T(8,128)}, f32[2,64,512]{2,1,0:T(8,128)}, u32[]{:S(2)}, u32[]{:S(2)}) %collective-permute-start.8) | collective-permute-done | bytes 262176 | tf_op jit(solution)/shard_map/ppermute | solution.py:20
  123.0 1.8 fusion.47
  124.9 1.8 convolution_subtract_fusion.4
  126.8 1.8 fusion.48
  128.6 1.8 convolution_subtract_fusion.3
  130.5 2.1 fusion.49
  132.6 1.9 convolution_subtract_fusion.2
  135.3 3.3 constant_dynamic-update-slice_fusion.6
  138.6 27.6 %all-gather.5.cloned.1.call-done = f32[2,256,1024]{2,1,0:T(8,128)} async-done(((f32[2,64,1024]{2,1,0:T(8,128)}), f32[2,256,1024]{2,1,0:T(8,128)}) %all-gather.5.cloned.1.call-update) | async-done | bytes 2097168 | tf_op jit(solution)/shard_map/all_gather | solution.py:123
  166.2 3.3 constant_dynamic-update-slice_fusion.5
  169.5 7.3 %copy.26 = f32[2,256,2048]{1,0,2:T(2,128)} copy(f32[2,256,2048]{2,1,0:T(8,128)} %constant_dynamic-update-slice_fusion.5) | data formatting | bytes 8388608 | tf_op jit(solution)/shard_map/reshape | solution.py:129
  179.4 4.7 %convolution_subtract_fusion.1 = f32[192,2048]{1,0:T(8,128)S(1)} fusion(f32[192,512]{1,0:T(8,128)S(1)} %fusion.50, f32[512,2048]{1,0:T(8,128)} %bitcast.137, f32[192,1024]{1,0:T(8,128)S(1)} %bitcast.139, pred[]{:T(512)S(6)} %eq.100), kind=kOutput, calls=%fused_computation.8 | convolution fusion | flops 2416705536 | bytes 6946817 | tf_op jit(solution)/shard_map/dot_general | solution.py:39
  185.0 39.9 %all-reduce.7.cloned.1.call-done = f32[512,256]{1,0:T(8,128)} async-done(((f32[512,256]{1,0:T(8,128)}), f32[512,256]{1,0:T(8,128)}) %all-reduce.7.cloned.1.call-update) | async-done | bytes 524304 | tf_op jit(solution)/shard_map/psum | solution.py:156
  224.9 1.8 multiply_add_fusion
  237.6 51.7 %collective-permute-done.12 = f32[8,64,256]{2,1,0:T(8,128)} collective-permute-done((f32[8,64,256]{2,1,0:T(8,128)}, f32[8,64,256]{2,1,0:T(8,128)}, u32[]{:S(2)}, u32[]{:S(2)}) %collective-permute-start.12) | collective-permute-done | bytes 524320 | tf_op jit(solution)/shard_map/ppermute | solution.py:35
  290.4 9.7 %collective-permute-done.14 = f32[512,256]{1,0:T(8,128)} collective-permute-done((f32[512,256]{1,0:T(8,128)}, f32[512,256]{1,0:T(8,128)}, u32[]{:S(2)}, u32[]{:S(2)}) %collective-permute-start.14) | collective-permute-done | bytes 524320 | tf_op jit(solution)/shard_map/ppermute | solution.py:35
  300.1 2.2 convolution_negate_fusion
  304.5 43.1 %all-reduce.9.cloned.1.call-done = f32[256,256]{1,0:T(8,128)} async-done(((f32[256,256]{1,0:T(8,128)}), f32[256,256]{1,0:T(8,128)}) %all-reduce.9.cloned.1.call-update) | async-done | bytes 262160 | tf_op jit(solution)/shard_map/psum | solution.py:173
  347.6 2.5 dynamic-slice_add_fusion
  354.3 2.3 dynamic-slice_add_fusion.1
  (151 shorter events, 57.6 us)
Async XLA Ops:
  7.2 1.2 copy-start
  7.2 128.2 %all-gather.3.cloned.1.call-start = ((), (), s32[]{:S(2)}) async-start(), calls=%async_computation | async-start | bytes 2621440 | tf_op jit(solution)/shard_map/all_gather | solution.py:122
  10.3 2.7 collective-permute-start
  13.1 29.1 %collective-permute-start.2 = (f32[1,64,256]{2,1,0:T(8,128)S(1)}, f32[1,64,256]{2,1,0:T(8,128)S(1)}, u32[]{:S(2)}, u32[]{:S(2)}) collective-permute-start(f32[1,64,256]{2,1,0:T(8,128)S(1)} %get-tuple-element.13), channel_id=1, source_target_pairs={{0,3},{1,0},{2,1},{3,2},{4,7},{5,4},{6,5},{7,6},{8,11},{9,8},{10,9... | collective-permute-start | bytes 196616 | tf_op jit(solution)/shard_map/ppermute | solution.py:25
  16.6 23.9 %collective-permute-start.1 = (f32[1,64,256]{2,1,0:T(8,128)S(1)}, f32[1,64,256]{2,1,0:T(8,128)S(1)}, u32[]{:S(2)}, u32[]{:S(2)}) collective-permute-start(f32[1,64,256]{2,1,0:T(8,128)S(1)} %get-tuple-element.13), channel_id=1, source_target_pairs={{0,1},{1,2},{2,3},{3,0},{4,5},{5,6},{6,7},{7,4},{8,9},{9,10},{10,1... | collective-permute-start | bytes 196616 | tf_op jit(solution)/shard_map/ppermute | solution.py:20
  40.5 10.1 %copy-start.4 = (f32[256,768]{1,0:T(8,128)}, f32[256,768]{1,0:T(8,128)S(1)}, u32[]{:S(2)}) copy-start(f32[256,768]{1,0:T(8,128)S(1)} %all_gather.12) | copy-start | bytes 2359300
  40.5 5.2 %collective-permute-start.3 = (f32[1,64,256]{2,1,0:T(8,128)S(1)}, f32[1,64,256]{2,1,0:T(8,128)S(1)}, u32[]{:S(2)}, u32[]{:S(2)}) collective-permute-start(f32[1,64,256]{2,1,0:T(8,128)S(1)} %collective-permute-done.1), channel_id=1, source_target_pairs={{0,1},{1,2},{2,3},{3,0},{4,5},{5,6},{6,7},{7,4},{8,9},{9,10},{10,1... | collective-permute-start | bytes 196616 | tf_op jit(solution)/shard_map/ppermute | solution.py:20
  48.7 1.9 copy-start.8
  58.3 45.6 %copy-start.3 = (f32[3,64,1536]{2,1,0:T(8,128)}, f32[3,64,1536]{2,1,0:T(8,128)S(1)}, u32[]{:S(2)}) copy-start(f32[3,64,1536]{2,1,0:T(8,128)S(1)} %broadcast_select_fusion) | copy-start | bytes 3538948
  59.1 2.4 collective-permute-start.4
  62.5 19.9 %collective-permute-start.5 = (f32[2,64,1536]{2,1,0:T(8,128)}, f32[2,64,1536]{2,1,0:T(8,128)}, u32[]{:S(2)}, u32[]{:S(2)}) collective-permute-start(f32[2,64,1536]{2,1,0:T(8,128)} %fusion.92), channel_id=1, source_target_pairs={{0,8},{4,12},{8,0},{12,4},{16,24},{20,28},{24,16},{28,20},{1,9},{5... | collective-permute-start | bytes 2359304 | tf_op jit(solution)/shard_map/ppermute | solution.py:35
  64.1 22.5 %copy-start.9 = (f32[2,64,256]{2,1,0:T(8,128)S(1)}, f32[2,64,256]{2,1,0:T(8,128)}, u32[]{:S(2)}) copy-start(f32[2,64,256]{2,1,0:T(8,128)} %param.7) | copy-start | bytes 393220
  84.7 2.5 copy-start.7
  85.7 80.6 %all-gather.5.cloned.1.call-start = ((), (), s32[]{:S(2)}) async-start(), calls=%async_computation.1 | async-start | bytes 2621440 | tf_op jit(solution)/shard_map/all_gather | solution.py:123
  87.2 143.5 %collective-permute-start.11 = (f32[8,64,256]{2,1,0:T(8,128)}, f32[8,64,256]{2,1,0:T(8,128)}, u32[]{:S(2)}, u32[]{:S(2)}) collective-permute-start(f32[8,64,256]{2,1,0:T(8,128)} %constant_dynamic-update-slice_fusion), channel_id=1, source_target_pairs={{0,4},{4,0},{8,12},{12,8},{16,20},{20,16},{24,28},{28,24},{1,5},{5... | collective-permute-start | bytes 1572872 | tf_op jit(solution)/shard_map/ppermute | solution.py:35
  89.9 13.1 %collective-permute-start.6 = (f32[2,64,512]{2,1,0:T(8,128)}, f32[2,64,512]{2,1,0:T(8,128)}, u32[]{:S(2)}, u32[]{:S(2)}) collective-permute-start(f32[2,64,512]{2,1,0:T(8,128)} %get-tuple-element.5), channel_id=1, source_target_pairs={{0,1},{1,2},{2,3},{3,0},{4,5},{5,6},{6,7},{7,4},{8,9},{9,10},{10,1... | collective-permute-start | bytes 786440 | tf_op jit(solution)/shard_map/ppermute | solution.py:20
  93.9 17.9 %collective-permute-start.7 = (f32[2,64,512]{2,1,0:T(8,128)}, f32[2,64,512]{2,1,0:T(8,128)}, u32[]{:S(2)}, u32[]{:S(2)}) collective-permute-start(f32[2,64,512]{2,1,0:T(8,128)} %get-tuple-element.5), channel_id=1, source_target_pairs={{0,3},{1,0},{2,1},{3,2},{4,7},{5,4},{6,5},{7,6},{8,11},{9,8},{10,9... | collective-permute-start | bytes 786440 | tf_op jit(solution)/shard_map/ppermute | solution.py:25
  103.0 14.0 %collective-permute-start.8 = (f32[2,64,512]{2,1,0:T(8,128)}, f32[2,64,512]{2,1,0:T(8,128)}, u32[]{:S(2)}, u32[]{:S(2)}) collective-permute-start(f32[2,64,512]{2,1,0:T(8,128)} %collective-permute-done.6), channel_id=1, source_target_pairs={{0,1},{1,2},{2,3},{3,0},{4,5},{5,6},{6,7},{7,4},{8,9},{9,10},{10,1... | collective-permute-start | bytes 786440 | tf_op jit(solution)/shard_map/ppermute | solution.py:20
  105.9 118.9 %all-reduce.7.cloned.1.call-start = ((), (), s32[]{:S(2)}) async-start(), calls=%async_computation.2 | async-start | bytes 1048576 | tf_op jit(solution)/shard_map/psum | solution.py:156
  132.6 1.9 slice-start
  176.8 2.6 slice-start.1
  179.3 168.3 %all-reduce.9.cloned.1.call-start = ((), (), s32[]{:S(2)}) async-start(), calls=%async_computation.3 | async-start | bytes 524288 | tf_op jit(solution)/shard_map/psum | solution.py:173
  224.9 8.0 %collective-permute-start.13 = (f32[512,256]{1,0:T(8,128)}, f32[512,256]{1,0:T(8,128)S(1)}, u32[]{:S(2)}, u32[]{:S(2)}) collective-permute-start(f32[512,256]{1,0:T(8,128)} %all-reduce.7.cloned.1.call-done), channel_id=1, source_target_pairs={{0,4},{4,0},{8,12},{12,8},{16,20},{20,16},{24,28},{28,24},{1,5},{5... | collective-permute-start | bytes 1572872 | tf_op jit(solution)/shard_map/ppermute | solution.py:35
  226.7 2.6 copy-start.2
  226.7 6.2 %copy-start.10 = (f32[512,256]{1,0:T(8,128)S(1)}, f32[512,256]{1,0:T(8,128)}, u32[]{:S(2)}) copy-start(f32[512,256]{1,0:T(8,128)} %all-reduce.7.cloned.1.call-done) | copy-start | bytes 1572868
  226.7 8.6 %copy-start.5 = (f32[256,768]{1,0:T(8,128)S(1)}, f32[256,768]{1,0:T(8,128)}, u32[]{:S(2)}) copy-start(f32[256,768]{1,0:T(8,128)} %copy-done.4) | copy-start | bytes 2359300
  229.3 118.4 %collective-permute-start.9 = (f32[4,64,2048]{2,1,0:T(8,128)}, f32[4,64,2048]{2,1,0:T(8,128)}, u32[]{:S(2)}, u32[]{:S(2)}) collective-permute-start(f32[4,64,2048]{2,1,0:T(8,128)} %constant_dynamic-slice_fusion.3), channel_id=1, source_target_pairs={{0,8},{4,12},{8,0},{12,4},{16,24},{20,28},{24,16},{28,20},{1,9},{5... | collective-permute-start | bytes 6291464 | tf_op jit(solution)/shard_map/ppermute | solution.py:35
  232.3 57.0 %collective-permute-start.12 = (f32[8,64,256]{2,1,0:T(8,128)}, f32[8,64,256]{2,1,0:T(8,128)}, u32[]{:S(2)}, u32[]{:S(2)}) collective-permute-start(f32[8,64,256]{2,1,0:T(8,128)} %add_dynamic-update-slice_fusion), channel_id=1, source_target_pairs={{0,8},{4,12},{8,0},{12,4},{16,24},{20,28},{24,16},{28,20},{1,9},{5... | collective-permute-start | bytes 1572872 | tf_op jit(solution)/shard_map/ppermute | solution.py:35
  233.8 66.3 %collective-permute-start.14 = (f32[512,256]{1,0:T(8,128)}, f32[512,256]{1,0:T(8,128)}, u32[]{:S(2)}, u32[]{:S(2)}) collective-permute-start(f32[512,256]{1,0:T(8,128)} %add.320), channel_id=1, source_target_pairs={{0,8},{4,12},{8,0},{12,4},{16,24},{20,28},{24,16},{28,20},{1,9},{5... | collective-permute-start | bytes 1572872 | tf_op jit(solution)/shard_map/ppermute | solution.py:35
  347.6 4.1 %collective-permute-start.15 = (f32[256,256]{1,0:T(8,128)}, f32[256,256]{1,0:T(8,128)}, u32[]{:S(2)}, u32[]{:S(2)}) collective-permute-start(f32[256,256]{1,0:T(8,128)} %all-reduce.9.cloned.1.call-done), channel_id=1, source_target_pairs={{0,4},{4,0},{8,12},{12,8},{16,20},{20,16},{24,28},{28,24},{1,5},{5... | collective-permute-start | bytes 786440 | tf_op jit(solution)/shard_map/ppermute | solution.py:35
  351.2 3.1 collective-permute-start.10
  351.7 4.9 %copy-start.1 = (f32[4,64,1024]{2,1,0:T(8,128)S(1)}, f32[4,64,1024]{2,1,0:T(8,128)}, u32[]{:S(2)}) copy-start(f32[4,64,1024]{2,1,0:T(8,128)} %param.4) | copy-start | bytes 3145732
  (1 other events, 1.1 us)
Sparse Core Ops, SparseCore 0:
  85.8 42.4 all-gather.2
  130.7 35.4 all-gather.4
  179.4 45.3 all-reduce.6
  304.5 43.0 all-reduce.8
